TPU v7x, 512 devices: a whole 4x4x16 slice. The times are simulated.
512 devices in a mesh: rep: 2 (over core), row: 16 (over y, x), col: 16 (over z).
Axes of the slice: x: 4, y: 4, z: 16, core: 2. Of those that a mesh axis runs over, the one named last changes fastest.
Arguments:
- residual: bfloat16 [16384, 2048], P(('rep', 'row'), 'col'), may hold values from -6 to 6
- post_gain: float32 [2048], replicated, may hold values from 0.25 to 1.75
- w_gate: bfloat16 [2048, 6144], P('row', 'col'), may hold values from -0.125 to 0.125
- w_up: bfloat16 [2048, 6144], P('row', 'col'), may hold values from -0.125 to 0.125
- w_down: bfloat16 [6144, 2048], P('col', 'row'), may hold values from -0.078125 to 0.078125
- next_gain: float32 [2048], replicated, may hold values from 0.25 to 1.75
- w_qkv: bfloat16 [2048, 4096], P('row', 'col'), may hold values from -0.125 to 0.125
- q_gain: float32 [128], replicated, may hold values from 0.25 to 1.75
- k_gain: float32 [128], replicated, may hold values from 0.25 to 1.75
- source: int32 [16384], P(('rep', 'row')), may hold values from 0 to 16383, as said below
Outputs:
- moved_residual: bfloat16 [16384, 2048], P(('rep', 'row'), 'col')
- moved_qkv: bfloat16 [16384, 4096], P(('rep', 'row'), 'col')
Inputs may be any that keep to these rules, and one draw needn't show every extreme that they name: source is a permutation of all rows. Rows are grouped in blocks of 512 (block b holds rows b * 512 to (b + 1) * 512 - 1, blocks of replica 0 first); output block b takes its rows from input block b or from the block of the same row index in the other replica, at most 128 of them from the other replica, and some block takes exactly 128. A block takes as many rows from the other replica as it gives to it.
All inputs are finite; a program needn't handle non-finite values.
Results may differ from a plain program's by a relative error of at most 0.0065.
Values may be sent and summed in bfloat16 or wider, within the bound.
A program may use at most 64 MiB of HBM per device.

v0:
```python
import jax
import jax.numpy as jnp
from jax import lax
from jax.sharding import PartitionSpec as P

HEADS = 16
KV_HEADS = 8
HD = 128
epsilon = 1e-06


def swapped(x, axis, apart):
    return lax.ppermute(x, axis, [(i, i ^ 1 << apart) for i in range(lax.axis_size(axis))])


def normalize(values, gain):
    scale = lax.rsqrt(jnp.mean(values * values, axis=-1, keepdims=True) + epsilon)
    return values * scale * gain


def per_device(residual, post_gain, w_gate, w_up, w_down, next_gain, w_qkv, q_gain, k_gain, source):
    tok_rows = residual.shape[0]
    col_index = lax.axis_index("col")
    gathered = lax.all_gather(residual, "col", axis=1, tiled=True)
    stream = gathered.astype(jnp.float32)
    normed = normalize(stream, post_gain).astype(jnp.bfloat16)
    columns = normed
    gate_proj = jnp.dot(
        columns,
        lax.all_gather(w_gate, "row", axis=0, tiled=True),
        preferred_element_type=jnp.float32,
    )
    up_proj = jnp.dot(
        columns, lax.all_gather(w_up, "row", axis=0, tiled=True), preferred_element_type=jnp.float32
    )
    hidden = (jax.nn.silu(gate_proj) * up_proj).astype(jnp.bfloat16)
    partial_value = jnp.dot(
        hidden,
        lax.all_gather(w_down, "row", axis=1, tiled=True),
        preferred_element_type=jnp.float32,
    )
    mlp_share = lax.psum_scatter(partial_value, "col", scatter_dimension=1, tiled=True)
    resid_own = (residual.astype(jnp.float32) + mlp_share).astype(jnp.bfloat16)
    resid_full = lax.all_gather(resid_own, "col", axis=1, tiled=True)
    next_normed = normalize(resid_full.astype(jnp.float32), next_gain).astype(jnp.bfloat16)
    proj_width = w_qkv.shape[1]
    columns = next_normed
    projected = jnp.dot(
        columns,
        lax.all_gather(w_qkv, "row", axis=0, tiled=True),
        preferred_element_type=jnp.float32,
    )
    head_count = proj_width // HD
    per_head = projected.reshape(tok_rows, head_count, HD)
    head_number = col_index * head_count + jnp.arange(head_count, dtype=jnp.int32)
    is_query = head_number < HEADS
    is_key = jnp.logical_and(head_number >= HEADS, head_number < HEADS + KV_HEADS)
    head_gain = jnp.where(is_query[:, None], q_gain[None, :], k_gain[None, :])
    head_scaled = normalize(per_head, head_gain)
    keep_norm = jnp.logical_or(is_query, is_key)[None, :, None]
    qkv_own = (
        jnp.where(keep_norm, head_scaled, per_head)
        .reshape(tok_rows, proj_width)
        .astype(jnp.bfloat16)
    )
    my_block = lax.axis_index("rep") * lax.axis_size("row") + lax.axis_index("row")
    from_peer = source // tok_rows != my_block
    local_row = source % tok_rows
    peer_resid, peer_qkv = swapped((resid_own, qkv_own), "rep", 0)
    picked = local_row + tok_rows * from_peer.astype(jnp.int32)
    moved_residual = jnp.take(jnp.concatenate([resid_own, peer_resid], axis=0), picked, axis=0)
    moved_qkv = jnp.take(jnp.concatenate([qkv_own, peer_qkv], axis=0), picked, axis=0)
    return (moved_residual, moved_qkv)


def solution(mesh):
    return jax.shard_map(
        per_device,
        mesh=mesh,
        in_specs=(
            P(("rep", "row"), "col"),
            P(),
            P("row", "col"),
            P("row", "col"),
            P("col", "row"),
            P(),
            P("row", "col"),
            P(),
            P(),
            P(("rep", "row")),
        ),
        out_specs=(P(("rep", "row"), "col"), P(("rep", "row"), "col")),
        check_vma=False,
    )
```

profile of v0, /device:TPU:1, one launch (start us, length us, event | category | flops | bytes accessed | tf_op | source)
XLA Modules:
  0.0 517.1 jit_solution(11629037548047053310)
XLA Ops:
  7.2 0.7 all-gather.7.cloned.1.call-update
  8.0 0.7 all-gather.9.cloned.1.call-update
  8.7 0.7 all-gather.11.cloned.1.call-update
  9.4 0.5 all-gather.13.cloned.1.call-update
  10.0 74.2 %all-gather.7.cloned.1.call-done = bf16[512,2048]{1,0:T(8,128)(2,1)} async-done(((bf16[512,128]{1,0:T(8,128)(2,1)}), bf16[512,2048]{1,0:T(8,128)(2,1)}) %all-gather.7.cloned.1.call-update) | async-done | bytes 2097168 | tf_op jit(solution)/shard_map/all_gather | solution.py:24
  84.2 2.2 fusion
  86.4 65.4 %all-gather.9.cloned.1.call-done = bf16[2048,384]{1,0:T(8,128)(2,1)} async-done(((bf16[128,384]{1,0:T(8,128)(2,1)}), bf16[2048,384]{1,0:T(8,128)(2,1)}) %all-gather.9.cloned.1.call-update) | async-done | bytes 1572880 | tf_op jit(solution)/shard_map/all_gather | solution.py:30
  151.8 2.7 fusion.19
  154.5 59.1 %all-gather.11.cloned.1.call-done = bf16[2048,384]{1,0:T(8,128)(2,1)} async-done(((bf16[128,384]{1,0:T(8,128)(2,1)}), bf16[2048,384]{1,0:T(8,128)(2,1)}) %all-gather.11.cloned.1.call-update) | async-done | bytes 1572880 | tf_op jit(solution)/shard_map/all_gather | solution.py:34
  213.6 62.7 %all-gather.13.cloned.1.call-done = bf16[384,2048]{1,0:T(8,128)(2,1)} async-done(((bf16[384,128]{1,0:T(8,128)(2,1)}), bf16[384,2048]{1,0:T(8,128)(2,1)}) %all-gather.13.cloned.1.call-update) | async-done | bytes 1572880 | tf_op jit(solution)/shard_map/all_gather | solution.py:39
  276.3 6.2 %fusion.11 = f32[512,2048]{1,0:T(8,128)} fusion(bf16[384,2048]{1,0:T(8,128)(2,1)} %all-gather.13.cloned.1.call-done, bf16[2048,384]{1,0:T(8,128)(2,1)} %all-gather.11.cloned.1.call-done, f32[512,384]{1,0:T(8,128)S(1)} %fusion.19, bf16[512,2048]{1,0:T(8,128)(2,1)S(1)} %copy-done.1, f32[2048]{0:T(1024)S(1)} %copy-done.7, f32[512]{0:T(512)S(1)} %add_rsqrt_fusion.2), kind=kOutput, calls=%fused_computation.17 | convolution fusion | flops 1615986688 | bytes 10233856 | tf_op jit(solution)/shard_map/dot_general | solution.py:37
  282.6 71.0 %reduce-scatter.2.cloned.1.call-done = f32[512,128]{1,0:T(8,128)} async-done(((f32[512,2048]{1,0:T(8,128)}), f32[512,128]{1,0:T(8,128)}) %reduce-scatter.2.cloned.1.call-update) | async-done | bytes 262160 | tf_op jit(solution)/shard_map/reduce_scatter | solution.py:42
  353.6 1.6 add_convert_fusion
  355.3 0.7 all-gather.17.cloned.1.call-update
  356.3 11.9 %collective-permute-start = (bf16[512,128]{1,0:T(8,128)(2,1)}, bf16[512,128]{1,0:T(8,128)(2,1)S(1)}, u32[]{:S(2)}, u32[]{:S(2)}) collective-permute-start(bf16[512,128]{1,0:T(8,128)(2,1)} %add_convert_fusion), channel_id=1, source_target_pairs={{0,256},{256,0},{1,257},{257,1},{2,258},{258,2},{3,259},{259,3},{4... | collective-permute-start | bytes 393224 | tf_op jit(solution)/shard_map/ppermute | solution.py:13
  368.2 64.5 %all-gather.15.cloned.1.call-done = bf16[512,2048]{1,0:T(8,128)(2,1)} async-done(((bf16[512,128]{1,0:T(8,128)(2,1)}), bf16[512,2048]{1,0:T(8,128)(2,1)}) %all-gather.15.cloned.1.call-update) | async-done | bytes 2097168 | tf_op jit(solution)/shard_map/all_gather | solution.py:44
  432.6 2.2 fusion.3
  434.9 63.7 %all-gather.17.cloned.1.call-done = bf16[2048,256]{1,0:T(8,128)(2,1)} async-done(((bf16[128,256]{1,0:T(8,128)(2,1)}), bf16[2048,256]{1,0:T(8,128)(2,1)}) %all-gather.17.cloned.1.call-update) | async-done | bytes 1048592 | tf_op jit(solution)/shard_map/all_gather | solution.py:50
  498.6 2.2 bitcast_reduce_fusion
  500.9 4.0 collective-permute-start.1
  505.0 1.3 gather_fusion
  506.3 0.8 broadcast_select_fusion.1
  507.4 2.0 gather_fusion.1
  509.4 0.8 broadcast_select_fusion
  (41 shorter events, 1.0 us)
Async XLA Ops:
  7.2 144.7 %copy-start.7 = (f32[2048]{0:T(1024)S(1)}, f32[2048]{0:T(1024)}, u32[]{:S(2)}) copy-start(f32[2048]{0:T(1024)} %param.11) | copy-start | bytes 24580
  7.2 77.0 %all-gather.7.cloned.1.call-start = ((), (), s32[]{:S(2)}) async-start(), calls=%async_computation.1 | async-start | bytes 2228224 | tf_op jit(solution)/shard_map/all_gather | solution.py:24
  7.9 143.9 %all-gather.9.cloned.1.call-start = ((), (), s32[]{:S(2)}) async-start(), calls=%async_computation.2 | async-start | bytes 1671168 | tf_op jit(solution)/shard_map/all_gather | solution.py:30
  8.7 204.9 %all-gather.11.cloned.1.call-start = ((), (), s32[]{:S(2)}) async-start(), calls=%async_computation.3 | async-start | bytes 1671168 | tf_op jit(solution)/shard_map/all_gather | solution.py:34
  9.4 266.9 %all-gather.13.cloned.1.call-start = ((), (), s32[]{:S(2)}) async-start(), calls=%async_computation.4 | async-start | bytes 1671168 | tf_op jit(solution)/shard_map/all_gather | solution.py:39
  10.0 343.7 %reduce-scatter.2.cloned.1.call-start = ((), (), s32[]{:S(2)}) async-start(), calls=%async_computation.5 | async-start | bytes 4456448 | tf_op jit(solution)/shard_map/reduce_scatter | solution.py:42
  84.2 67.6 %copy-start.1 = (bf16[512,2048]{1,0:T(8,128)(2,1)S(1)}, bf16[512,2048]{1,0:T(8,128)(2,1)}, u32[]{:S(2)}) copy-start(bf16[512,2048]{1,0:T(8,128)(2,1)} %all-gather.7.cloned.1.call-done) | copy-start | bytes 6291460
  282.5 71.1 %copy-start.3 = (bf16[512,128]{1,0:T(8,128)(2,1)S(1)}, bf16[512,128]{1,0:T(8,128)(2,1)}, u32[]{:S(2)}) copy-start(bf16[512,128]{1,0:T(8,128)(2,1)} %param.10) | copy-start | bytes 393220
  282.6 73.5 %copy-start.4 = (s32[512]{0:T(512)S(1)}, s32[512]{0:T(512)}, u32[]{:S(2)}) copy-start(s32[512]{0:T(512)} %param.19) | copy-start | bytes 6148
  282.6 73.6 %copy-start.5 = (f32[128]{0:T(128)S(1)}, f32[128]{0:T(128)}, u32[]{:S(2)}) copy-start(f32[128]{0:T(128)} %param.18) | copy-start | bytes 1540
  282.6 73.6 %copy-start.6 = (f32[128]{0:T(128)S(1)}, f32[128]{0:T(128)}, u32[]{:S(2)}) copy-start(f32[128]{0:T(128)} %param.17) | copy-start | bytes 1540
  282.6 216.0 %copy-start.8 = (f32[2048]{0:T(1024)S(1)}, f32[2048]{0:T(1024)}, u32[]{:S(2)}) copy-start(f32[2048]{0:T(1024)} %param.15) | copy-start | bytes 24580
  282.6 150.0 %all-gather.15.cloned.1.call-start = ((), (), s32[]{:S(2)}) async-start(), calls=%async_computation.6 | async-start | bytes 2228224 | tf_op jit(solution)/shard_map/all_gather | solution.py:44
  355.3 143.3 %all-gather.17.cloned.1.call-start = ((), (), s32[]{:S(2)}) async-start(), calls=%async_computation.7 | async-start | bytes 1114112 | tf_op jit(solution)/shard_map/all_gather | solution.py:50
  356.3 148.7 %collective-permute-start = (bf16[512,128]{1,0:T(8,128)(2,1)}, bf16[512,128]{1,0:T(8,128)(2,1)S(1)}, u32[]{:S(2)}, u32[]{:S(2)}) collective-permute-start(bf16[512,128]{1,0:T(8,128)(2,1)} %add_convert_fusion), channel_id=1, source_target_pairs={{0,256},{256,0},{1,257},{257,1},{2,258},{258,2},{3,259},{259,3},{4... | collective-permute-start | bytes 393224 | tf_op jit(solution)/shard_map/ppermute | solution.py:13
  432.6 65.9 %copy-start = (bf16[512,2048]{1,0:T(8,128)(2,1)S(1)}, bf16[512,2048]{1,0:T(8,128)(2,1)}, u32[]{:S(2)}) copy-start(bf16[512,2048]{1,0:T(8,128)(2,1)} %all-gather.15.cloned.1.call-done) | copy-start | bytes 6291460
  434.9 70.1 %copy-start.2 = (bf16[512,128]{1,0:T(8,128)(2,1)S(1)}, bf16[512,128]{1,0:T(8,128)(2,1)}, u32[]{:S(2)}) copy-start(bf16[512,128]{1,0:T(8,128)(2,1)} %add_convert_fusion) | copy-start | bytes 393220
  500.9 6.2 %collective-permute-start.1 = (bf16[512,256]{0,1:T(8,128)(2,1)S(1)}, bf16[512,256]{0,1:T(8,128)(2,1)S(1)}, u32[]{:S(2)}, u32[]{:S(2)}) collective-permute-start(bf16[512,256]{0,1:T(8,128)(2,1)S(1)} %fusion.23), channel_id=1, source_target_pairs={{0,256},{256,0},{1,257},{257,1},{2,258},{258,2},{3,259},{259,3},{4... | collective-permute-start | bytes 786440 | tf_op jit(solution)/shard_map/ppermute | solution.py:13
Sparse Core Ops, SparseCore 0:
  10.0 74.1 all-gather.6
  87.2 64.5 all-gather.8
  154.8 58.7 all-gather.10
  216.4 59.8 all-gather.12
  282.7 70.8 reduce-scatter.1
  356.1 76.5 all-gather.14
  435.7 62.8 all-gather.16
where the time goes:
time: 517 us
  waiting for transfers between devices  464 us (90%)
  starting transfers between devices  16.2 us (3%)
  between operations  14.3 us (3%)
  matrix products  11.1 us (2%)
  other arithmetic  8.07 us (2%)
    all_gather x1, waiting for transfers between devices, per_device(): gathered = lax.all_gather(residual, 'col', axis=1, tiled=True)  74.2 us
    reduce_scatter x1, waiting for transfers between devices, per_device(): lax.psum_scatter(partial_value, 'col', scatter_dimension=1, tiled=True)  71 us
    all_gather x1, waiting for transfers between devices, per_device(): lax.all_gather(w_gate, 'row', axis=0, tiled=True)  65.4 us
    all_gather x1, waiting for transfers between devices, per_device(): resid_full = lax.all_gather(resid_own, 'col', axis=1, tiled=True)  64.5 us
    all_gather x1, waiting for transfers between devices, per_device(): lax.all_gather(w_qkv, 'row', axis=0, tiled=True)  63.7 us
    all_gather x1, waiting for transfers between devices, per_device(): lax.all_gather(w_down, 'row', axis=1, tiled=True)  62.7 us
    all_gather x1, waiting for transfers between devices, per_device(): lax.all_gather(w_up, 'row', axis=0, tiled=True)  59.1 us
    ppermute x2, starting transfers between devices, swapped(): lax.ppermute(x, axis, [(i, i ^ 1 << apart) for i in range(lax.axis_size(a...  15.9 us
  transfers between devices with their start and end apart: 9, of which 7 were waited for; matrix products, arithmetic and copies ran while one was open for 2% of the time, Pallas kernels for 0%

commit v1 on v0

--- a/solution.py
+++ b/solution.py
@@ -7,6 +7,22 @@
 KV_HEADS = 8
 HD = 128
 epsilon = 1e-06
+
+
+def balance_the_patch(body):
+    bus_axis = "row"
+    full_n = jax.lax.axis_size(bus_axis)
+    in_order = [(c, (c + 1) % full_n) for c in range(full_n)]
+    xs_all = [(c, (c - 1) % full_n) for c in range(full_n)]
+    clean, tile_out = ([body], [body])
+    for _ in range(full_n // 2):
+        clean.append(jax.lax.ppermute(clean[-1], bus_axis, in_order))
+    ix = 0
+    while ix < (full_n - 1) // 2:
+        tile_out.append(jax.lax.ppermute(tile_out[-1], bus_axis, xs_all))
+        ix = ix + 1
+    z2 = jnp.concatenate([*clean[::-1], *tile_out[1:]], axis=1)
+    return jnp.roll(z2, (jax.lax.axis_index(bus_axis) - full_n // 2) * body.shape[1], axis=1)
 
 
 def swapped(x, axis, apart):
@@ -34,11 +50,7 @@
         columns, lax.all_gather(w_up, "row", axis=0, tiled=True), preferred_element_type=jnp.float32
     )
     hidden = (jax.nn.silu(gate_proj) * up_proj).astype(jnp.bfloat16)
-    partial_value = jnp.dot(
-        hidden,
-        lax.all_gather(w_down, "row", axis=1, tiled=True),
-        preferred_element_type=jnp.float32,
-    )
+    partial_value = jnp.dot(hidden, balance_the_patch(w_down), preferred_element_type=jnp.float32)
     mlp_share = lax.psum_scatter(partial_value, "col", scatter_dimension=1, tiled=True)
     resid_own = (residual.astype(jnp.float32) + mlp_share).astype(jnp.bfloat16)
     resid_full = lax.all_gather(resid_own, "col", axis=1, tiled=True)

time: 517 us -> 455 us (0.88)
  waiting for transfers between devices: 464 us -> 312 us
  starting transfers between devices: 16.2 us -> 81.3 us
  local copies, waits for them, and re-layouts: 3.61 us -> 25.9 us
    all_gather x1, waiting for transfers between devices: 74.2 us -> 0.01 us  [per_device(): gathered = lax.all_gather(residual, 'col', axis=1, tiled=True)]
    ppermute x0 -> x15, starting transfers between devices: none -> 64.8 us  [the longest x7 47.5 us: balance_the_patch(): tile_out.append(jax.lax.ppermute(tile_out[-1], bus_axis, xs_all))]
    all_gather x1 -> x0, waiting for transfers between devices: 62.7 us -> none  [per_device(): lax.all_gather(w_down, 'row', axis=1, tiled=True)]
    unnamed x18 -> x49, local copies, waits for them, and re-layouts: 0.04 us -> 21.7 us
    all_gather x1, waiting for transfers between devices: 65.4 us -> 45.9 us  [per_device(): lax.all_gather(w_gate, 'row', axis=0, tiled=True)]
    ppermute x0 -> x15, waiting for transfers between devices: none -> 7.2 us  [the longest x8 7.18 us: balance_the_patch(): clean.append(jax.lax.ppermute(clean[-1], bus_axis, in_order))]
  transfers between devices with their start and end apart: 9 -> 23, of which waited for: 7 -> 11; matrix products, arithmetic and copies ran while one was open for 2% -> 8% of each run, Pallas kernels for 0% -> 0%
where the time goes in v1:
time: 455 us; the launch traced here: 454 us
  waiting for transfers between devices  312 us (69%)
  starting transfers between devices  81.3 us (18%)
  local copies, waits for them, and re-layouts  25.9 us (6%)
  between operations  14.5 us (3%)
  matrix products  12.4 us (3%)
  other arithmetic  7.77 us (2%)
    reduce_scatter x1, waiting for transfers between devices, per_device(): lax.psum_scatter(partial_value, 'col', scatter_dimension=1, tiled=True)  70.7 us
    all_gather x1, waiting for transfers between devices, per_device(): resid_full = lax.all_gather(resid_own, 'col', axis=1, tiled=True)  64.1 us
    all_gather x1, waiting for transfers between devices, per_device(): lax.all_gather(w_qkv, 'row', axis=0, tiled=True)  63.7 us
    all_gather x1, waiting for transfers between devices, per_device(): lax.all_gather(w_up, 'row', axis=0, tiled=True)  58.4 us
    ppermute x7, starting transfers between devices, balance_the_patch(): tile_out.append(jax.lax.ppermute(tile_out[-1], bus_axis, xs_all))  47.5 us
    all_gather x1, waiting for transfers between devices, per_device(): lax.all_gather(w_gate, 'row', axis=0, tiled=True)  45.9 us
    unnamed x49, local copies, waits for them, and re-layouts  21.7 us
    ppermute x8, starting transfers between devices, balance_the_patch(): clean.append(jax.lax.ppermute(clean[-1], bus_axis, in_order))  17.3 us
  transfers between devices with their start and end apart: 23, of which 11 were waited for; matrix products, arithmetic and copies ran while one was open for 8% of the time, Pallas kernels for 0%

profile of v1, /device:TPU:1, one launch (start us, length us, event | category | flops | bytes accessed | tf_op | source)
XLA Modules:
  0.0 453.8 jit_solution(6958949865879156038)
XLA Ops:
  8.7 4.0 collective-permute-start
  12.7 5.9 %collective-permute-done = bf16[384,128]{1,0:T(8,128)(2,1)S(1)} collective-permute-done((bf16[384,128]{1,0:T(8,128)(2,1)}, bf16[384,128]{1,0:T(8,128)(2,1)S(1)}, u32[]{:S(2)}, u32[]{:S(2)}) %collective-permute-start) | collective-permute-done | bytes 98336 | tf_op jit(solution)/shard_map/ppermute | solution.py:19
  20.5 6.7 %collective-permute-start.8 = (bf16[384,128]{1,0:T(8,128)(2,1)}, bf16[384,128]{1,0:T(8,128)(2,1)S(1)}, u32[]{:S(2)}, u32[]{:S(2)}) collective-permute-start(bf16[384,128]{1,0:T(8,128)(2,1)} %param.14), channel_id=1, source_target_pairs={{0,240},{16,0},{32,16},{48,32},{64,48},{80,64},{96,80},{112,96},{1... | collective-permute-start | bytes 294920 | tf_op jit(solution)/shard_map/ppermute | solution.py:22
  29.2 6.9 %collective-permute-start.9 = (bf16[384,128]{1,0:T(8,128)(2,1)S(1)}, bf16[384,128]{1,0:T(8,128)(2,1)S(1)}, u32[]{:S(2)}, u32[]{:S(2)}) collective-permute-start(bf16[384,128]{1,0:T(8,128)(2,1)S(1)} %collective-permute-done.8), channel_id=1, source_target_pairs={{0,240},{16,0},{32,16},{48,32},{64,48},{80,64},{96,80},{112,96},{1... | collective-permute-start | bytes 294920 | tf_op jit(solution)/shard_map/ppermute | solution.py:22
  36.1 1.9 collective-permute-start.3
  38.0 6.9 %collective-permute-start.10 = (bf16[384,128]{1,0:T(8,128)(2,1)S(1)}, bf16[384,128]{1,0:T(8,128)(2,1)S(1)}, u32[]{:S(2)}, u32[]{:S(2)}) collective-permute-start(bf16[384,128]{1,0:T(8,128)(2,1)S(1)} %collective-permute-done.9), channel_id=1, source_target_pairs={{0,240},{16,0},{32,16},{48,32},{64,48},{80,64},{96,80},{112,96},{1... | collective-permute-start | bytes 294920 | tf_op jit(solution)/shard_map/ppermute | solution.py:22
  47.7 7.0 %collective-permute-start.11 = (bf16[384,128]{1,0:T(8,128)(2,1)S(1)}, bf16[384,128]{1,0:T(8,128)(2,1)S(1)}, u32[]{:S(2)}, u32[]{:S(2)}) collective-permute-start(bf16[384,128]{1,0:T(8,128)(2,1)S(1)} %collective-permute-done.10), channel_id=1, source_target_pairs={{0,240},{16,0},{32,16},{48,32},{64,48},{80,64},{96,80},{112,96},{1... | collective-permute-start | bytes 294920 | tf_op jit(solution)/shard_map/ppermute | solution.py:22
  54.9 1.9 collective-permute-start.5
  56.8 6.7 %collective-permute-start.12 = (bf16[384,128]{1,0:T(8,128)(2,1)S(1)}, bf16[384,128]{1,0:T(8,128)(2,1)S(1)}, u32[]{:S(2)}, u32[]{:S(2)}) collective-permute-start(bf16[384,128]{1,0:T(8,128)(2,1)S(1)} %collective-permute-done.11), channel_id=1, source_target_pairs={{0,240},{16,0},{32,16},{48,32},{64,48},{80,64},{96,80},{112,96},{1... | collective-permute-start | bytes 294920 | tf_op jit(solution)/shard_map/ppermute | solution.py:22
  65.5 6.7 %collective-permute-start.13 = (bf16[384,128]{1,0:T(8,128)(2,1)S(1)}, bf16[384,128]{1,0:T(8,128)(2,1)S(1)}, u32[]{:S(2)}, u32[]{:S(2)}) collective-permute-start(bf16[384,128]{1,0:T(8,128)(2,1)S(1)} %collective-permute-done.12), channel_id=1, source_target_pairs={{0,240},{16,0},{32,16},{48,32},{64,48},{80,64},{96,80},{112,96},{1... | collective-permute-start | bytes 294920 | tf_op jit(solution)/shard_map/ppermute | solution.py:22
  74.3 6.7 %collective-permute-start.14 = (bf16[384,128]{1,0:T(8,128)(2,1)S(1)}, bf16[384,128]{1,0:T(8,128)(2,1)S(1)}, u32[]{:S(2)}, u32[]{:S(2)}) collective-permute-start(bf16[384,128]{1,0:T(8,128)(2,1)S(1)} %collective-permute-done.13), channel_id=1, source_target_pairs={{0,240},{16,0},{32,16},{48,32},{64,48},{80,64},{96,80},{112,96},{1... | collective-permute-start | bytes 294920 | tf_op jit(solution)/shard_map/ppermute | solution.py:22
  103.3 2.1 fusion
  105.4 45.9 %all-gather.8.cloned.1.call-done = bf16[2048,384]{1,0:T(8,128)(2,1)} async-done(((bf16[128,384]{1,0:T(8,128)(2,1)}), bf16[2048,384]{1,0:T(8,128)(2,1)}) %all-gather.8.cloned.1.call-update) | async-done | bytes 1572880 | tf_op jit(solution)/shard_map/all_gather | solution.py:46
  151.3 3.3 fusion.20
  154.6 58.4 %all-gather.10.cloned.1.call-done = bf16[2048,384]{1,0:T(8,128)(2,1)} async-done(((bf16[128,384]{1,0:T(8,128)(2,1)}), bf16[2048,384]{1,0:T(8,128)(2,1)}) %all-gather.10.cloned.1.call-update) | async-done | bytes 1572880 | tf_op jit(solution)/shard_map/all_gather | solution.py:50
  213.1 6.3 %fusion.10 = f32[512,2048]{1,0:T(8,128)} fusion(bf16[384,4096]{1,0:T(8,128)(2,1)} %constant_dynamic-update-slice_fusion, s32[]{:T(128)S(6)} %select_n.55, bf16[2048,384]{1,0:T(8,128)(2,1)} %all-gather.10.cloned.1.call-done, f32[512,384]{1,0:T(8,128)S(1)} %fusion.20, bf16[512,2048]{1,0:T(8,128)(2,1)S(1)} %copy-done, f32[2048]{0:T(1024)S(1)} %copy-done.7, ...), kind=kOutput, calls=%fused_computation.15 | convolution fusion | flops 1615986688 | bytes 10233860 | tf_op jit(solution)/shard_map/dot_general | solution.py:53
  219.4 70.7 %reduce-scatter.2.cloned.1.call-done = f32[512,128]{1,0:T(8,128)} async-done(((f32[512,2048]{1,0:T(8,128)}), f32[512,128]{1,0:T(8,128)}) %reduce-scatter.2.cloned.1.call-update) | async-done | bytes 262160 | tf_op jit(solution)/shard_map/reduce_scatter | solution.py:54
  292.6 12.2 %collective-permute-start.15 = (bf16[512,128]{1,0:T(8,128)(2,1)}, bf16[512,128]{1,0:T(8,128)(2,1)S(1)}, u32[]{:S(2)}, u32[]{:S(2)}) collective-permute-start(bf16[512,128]{1,0:T(8,128)(2,1)} %add_convert_fusion), channel_id=1, source_target_pairs={{0,256},{256,0},{1,257},{257,1},{2,258},{258,2},{3,259},{259,3},{4... | collective-permute-start | bytes 393224 | tf_op jit(solution)/shard_map/ppermute | solution.py:29
  304.8 64.1 %all-gather.12.cloned.1.call-done = bf16[512,2048]{1,0:T(8,128)(2,1)} async-done(((bf16[512,128]{1,0:T(8,128)(2,1)}), bf16[512,2048]{1,0:T(8,128)(2,1)}) %all-gather.12.cloned.1.call-update) | async-done | bytes 2097168 | tf_op jit(solution)/shard_map/all_gather | solution.py:56
  368.9 2.1 fusion.3
  371.0 63.7 %all-gather.14.cloned.1.call-done = bf16[2048,256]{1,0:T(8,128)(2,1)} async-done(((bf16[128,256]{1,0:T(8,128)(2,1)}), bf16[2048,256]{1,0:T(8,128)(2,1)}) %all-gather.14.cloned.1.call-update) | async-done | bytes 1048592 | tf_op jit(solution)/shard_map/all_gather | solution.py:62
  434.7 2.8 bitcast_reduce_fusion
  437.6 4.0 collective-permute-start.16
  444.1 2.0 gather_fusion.1
  (100 shorter events, 40.6 us)
Async XLA Ops:
  7.2 96.1 %all-gather.6.cloned.1.call-start = ((), (), s32[]{:S(2)}) async-start(), calls=%async_computation.1 | async-start | bytes 2228224 | tf_op jit(solution)/shard_map/all_gather | solution.py:40
  7.9 143.4 %all-gather.8.cloned.1.call-start = ((), (), s32[]{:S(2)}) async-start(), calls=%async_computation.2 | async-start | bytes 1671168 | tf_op jit(solution)/shard_map/all_gather | solution.py:46
  8.7 204.4 %all-gather.10.cloned.1.call-start = ((), (), s32[]{:S(2)}) async-start(), calls=%async_computation.3 | async-start | bytes 1671168 | tf_op jit(solution)/shard_map/all_gather | solution.py:50
  8.7 9.9 %collective-permute-start = (bf16[384,128]{1,0:T(8,128)(2,1)}, bf16[384,128]{1,0:T(8,128)(2,1)S(1)}, u32[]{:S(2)}, u32[]{:S(2)}) collective-permute-start(bf16[384,128]{1,0:T(8,128)(2,1)} %param.14), channel_id=1, source_target_pairs={{0,16},{16,32},{32,48},{48,64},{64,80},{80,96},{96,112},{112,128},... | collective-permute-start | bytes 294920 | tf_op jit(solution)/shard_map/ppermute | solution.py:19
  18.6 8.7 %collective-permute-start.1 = (bf16[384,128]{1,0:T(8,128)(2,1)S(1)}, bf16[384,128]{1,0:T(8,128)(2,1)S(1)}, u32[]{:S(2)}, u32[]{:S(2)}) collective-permute-start(bf16[384,128]{1,0:T(8,128)(2,1)S(1)} %collective-permute-done), channel_id=1, source_target_pairs={{0,16},{16,32},{32,48},{48,64},{64,80},{80,96},{96,112},{112,128},... | collective-permute-start | bytes 294920 | tf_op jit(solution)/shard_map/ppermute | solution.py:19
  20.5 8.7 %collective-permute-start.8 = (bf16[384,128]{1,0:T(8,128)(2,1)}, bf16[384,128]{1,0:T(8,128)(2,1)S(1)}, u32[]{:S(2)}, u32[]{:S(2)}) collective-permute-start(bf16[384,128]{1,0:T(8,128)(2,1)} %param.14), channel_id=1, source_target_pairs={{0,240},{16,0},{32,16},{48,32},{64,48},{80,64},{96,80},{112,96},{1... | collective-permute-start | bytes 294920 | tf_op jit(solution)/shard_map/ppermute | solution.py:22
  27.3 8.8 %collective-permute-start.2 = (bf16[384,128]{1,0:T(8,128)(2,1)S(1)}, bf16[384,128]{1,0:T(8,128)(2,1)S(1)}, u32[]{:S(2)}, u32[]{:S(2)}) collective-permute-start(bf16[384,128]{1,0:T(8,128)(2,1)S(1)} %collective-permute-done.1), channel_id=1, source_target_pairs={{0,16},{16,32},{32,48},{48,64},{64,80},{80,96},{96,112},{112,128},... | collective-permute-start | bytes 294920 | tf_op jit(solution)/shard_map/ppermute | solution.py:19
  29.2 8.8 %collective-permute-start.9 = (bf16[384,128]{1,0:T(8,128)(2,1)S(1)}, bf16[384,128]{1,0:T(8,128)(2,1)S(1)}, u32[]{:S(2)}, u32[]{:S(2)}) collective-permute-start(bf16[384,128]{1,0:T(8,128)(2,1)S(1)} %collective-permute-done.8), channel_id=1, source_target_pairs={{0,240},{16,0},{32,16},{48,32},{64,48},{80,64},{96,80},{112,96},{1... | collective-permute-start | bytes 294920 | tf_op jit(solution)/shard_map/ppermute | solution.py:22
  36.1 9.6 %collective-permute-start.3 = (bf16[384,128]{1,0:T(8,128)(2,1)S(1)}, bf16[384,128]{1,0:T(8,128)(2,1)S(1)}, u32[]{:S(2)}, u32[]{:S(2)}) collective-permute-start(bf16[384,128]{1,0:T(8,128)(2,1)S(1)} %collective-permute-done.2), channel_id=1, source_target_pairs={{0,16},{16,32},{32,48},{48,64},{64,80},{80,96},{96,112},{112,128},... | collective-permute-start | bytes 294920 | tf_op jit(solution)/shard_map/ppermute | solution.py:19
  38.0 9.6 %collective-permute-start.10 = (bf16[384,128]{1,0:T(8,128)(2,1)S(1)}, bf16[384,128]{1,0:T(8,128)(2,1)S(1)}, u32[]{:S(2)}, u32[]{:S(2)}) collective-permute-start(bf16[384,128]{1,0:T(8,128)(2,1)S(1)} %collective-permute-done.9), channel_id=1, source_target_pairs={{0,240},{16,0},{32,16},{48,32},{64,48},{80,64},{96,80},{112,96},{1... | collective-permute-start | bytes 294920 | tf_op jit(solution)/shard_map/ppermute | solution.py:22
  45.7 9.2 %collective-permute-start.4 = (bf16[384,128]{1,0:T(8,128)(2,1)S(1)}, bf16[384,128]{1,0:T(8,128)(2,1)S(1)}, u32[]{:S(2)}, u32[]{:S(2)}) collective-permute-start(bf16[384,128]{1,0:T(8,128)(2,1)S(1)} %collective-permute-done.3), channel_id=1, source_target_pairs={{0,16},{16,32},{32,48},{48,64},{64,80},{80,96},{96,112},{112,128},... | collective-permute-start | bytes 294920 | tf_op jit(solution)/shard_map/ppermute | solution.py:19
  47.7 9.2 %collective-permute-start.11 = (bf16[384,128]{1,0:T(8,128)(2,1)S(1)}, bf16[384,128]{1,0:T(8,128)(2,1)S(1)}, u32[]{:S(2)}, u32[]{:S(2)}) collective-permute-start(bf16[384,128]{1,0:T(8,128)(2,1)S(1)} %collective-permute-done.10), channel_id=1, source_target_pairs={{0,240},{16,0},{32,16},{48,32},{64,48},{80,64},{96,80},{112,96},{1... | collective-permute-start | bytes 294920 | tf_op jit(solution)/shard_map/ppermute | solution.py:22
  54.9 8.7 %collective-permute-start.5 = (bf16[384,128]{1,0:T(8,128)(2,1)S(1)}, bf16[384,128]{1,0:T(8,128)(2,1)S(1)}, u32[]{:S(2)}, u32[]{:S(2)}) collective-permute-start(bf16[384,128]{1,0:T(8,128)(2,1)S(1)} %collective-permute-done.4), channel_id=1, source_target_pairs={{0,16},{16,32},{32,48},{48,64},{64,80},{80,96},{96,112},{112,128},... | collective-permute-start | bytes 294920 | tf_op jit(solution)/shard_map/ppermute | solution.py:19
  56.8 8.7 %collective-permute-start.12 = (bf16[384,128]{1,0:T(8,128)(2,1)S(1)}, bf16[384,128]{1,0:T(8,128)(2,1)S(1)}, u32[]{:S(2)}, u32[]{:S(2)}) collective-permute-start(bf16[384,128]{1,0:T(8,128)(2,1)S(1)} %collective-permute-done.11), channel_id=1, source_target_pairs={{0,240},{16,0},{32,16},{48,32},{64,48},{80,64},{96,80},{112,96},{1... | collective-permute-start | bytes 294920 | tf_op jit(solution)/shard_map/ppermute | solution.py:22
  63.6 8.7 %collective-permute-start.6 = (bf16[384,128]{1,0:T(8,128)(2,1)S(1)}, bf16[384,128]{1,0:T(8,128)(2,1)S(1)}, u32[]{:S(2)}, u32[]{:S(2)}) collective-permute-start(bf16[384,128]{1,0:T(8,128)(2,1)S(1)} %collective-permute-done.5), channel_id=1, source_target_pairs={{0,16},{16,32},{32,48},{48,64},{64,80},{80,96},{96,112},{112,128},... | collective-permute-start | bytes 294920 | tf_op jit(solution)/shard_map/ppermute | solution.py:19
  65.5 8.8 %collective-permute-start.13 = (bf16[384,128]{1,0:T(8,128)(2,1)S(1)}, bf16[384,128]{1,0:T(8,128)(2,1)S(1)}, u32[]{:S(2)}, u32[]{:S(2)}) collective-permute-start(bf16[384,128]{1,0:T(8,128)(2,1)S(1)} %collective-permute-done.12), channel_id=1, source_target_pairs={{0,240},{16,0},{32,16},{48,32},{64,48},{80,64},{96,80},{112,96},{1... | collective-permute-start | bytes 294920 | tf_op jit(solution)/shard_map/ppermute | solution.py:22
  72.3 8.7 %collective-permute-start.7 = (bf16[384,128]{1,0:T(8,128)(2,1)S(1)}, bf16[384,128]{1,0:T(8,128)(2,1)S(1)}, u32[]{:S(2)}, u32[]{:S(2)}) collective-permute-start(bf16[384,128]{1,0:T(8,128)(2,1)S(1)} %collective-permute-done.6), channel_id=1, source_target_pairs={{0,16},{16,32},{32,48},{48,64},{64,80},{80,96},{96,112},{112,128},... | collective-permute-start | bytes 294920 | tf_op jit(solution)/shard_map/ppermute | solution.py:19
  74.2 215.9 %reduce-scatter.2.cloned.1.call-start = ((), (), s32[]{:S(2)}) async-start(), calls=%async_computation.4 | async-start | bytes 4456448 | tf_op jit(solution)/shard_map/reduce_scatter | solution.py:54
  74.3 17.7 %collective-permute-start.14 = (bf16[384,128]{1,0:T(8,128)(2,1)S(1)}, bf16[384,128]{1,0:T(8,128)(2,1)S(1)}, u32[]{:S(2)}, u32[]{:S(2)}) collective-permute-start(bf16[384,128]{1,0:T(8,128)(2,1)S(1)} %collective-permute-done.13), channel_id=1, source_target_pairs={{0,240},{16,0},{32,16},{48,32},{64,48},{80,64},{96,80},{112,96},{1... | collective-permute-start | bytes 294920 | tf_op jit(solution)/shard_map/ppermute | solution.py:22
  219.3 215.3 %copy-start.8 = (f32[2048]{0:T(1024)S(1)}, f32[2048]{0:T(1024)}, u32[]{:S(2)}) copy-start(f32[2048]{0:T(1024)} %param.15) | copy-start | bytes 24580
  219.4 149.5 %all-gather.12.cloned.1.call-start = ((), (), s32[]{:S(2)}) async-start(), calls=%async_computation.5 | async-start | bytes 2228224 | tf_op jit(solution)/shard_map/all_gather | solution.py:56
  291.8 142.9 %all-gather.14.cloned.1.call-start = ((), (), s32[]{:S(2)}) async-start(), calls=%async_computation.6 | async-start | bytes 1114112 | tf_op jit(solution)/shard_map/all_gather | solution.py:62
  292.6 149.1 %collective-permute-start.15 = (bf16[512,128]{1,0:T(8,128)(2,1)}, bf16[512,128]{1,0:T(8,128)(2,1)S(1)}, u32[]{:S(2)}, u32[]{:S(2)}) collective-permute-start(bf16[512,128]{1,0:T(8,128)(2,1)} %add_convert_fusion), channel_id=1, source_target_pairs={{0,256},{256,0},{1,257},{257,1},{2,258},{258,2},{3,259},{259,3},{4... | collective-permute-start | bytes 393224 | tf_op jit(solution)/shard_map/ppermute | solution.py:29
  437.6 6.2 %collective-permute-start.16 = (bf16[512,256]{0,1:T(8,128)(2,1)S(1)}, bf16[512,256]{0,1:T(8,128)(2,1)S(1)}, u32[]{:S(2)}, u32[]{:S(2)}) collective-permute-start(bf16[512,256]{0,1:T(8,128)(2,1)S(1)} %fusion.24), channel_id=1, source_target_pairs={{0,256},{256,0},{1,257},{257,1},{2,258},{258,2},{3,259},{259,3},{4... | collective-permute-start | bytes 786440 | tf_op jit(solution)/shard_map/ppermute | solution.py:29
  (8 other events, 621.4 us)
Sparse Core Ops, SparseCore 0:
  10.0 74.3 all-gather.5
  87.4 63.8 all-gather.7
  154.3 58.7 all-gather.9
  219.5 70.5 reduce-scatter.1
  292.5 76.3 all-gather.11
  371.8 62.8 all-gather.13
